TPU v7x, 32 devices: a whole 2x2x4 slice. The times are simulated.
32 devices in a mesh: run: 8 (over z, y), rep: 4 (over x, core).
Axes of the slice: x: 2, y: 2, z: 4, core: 2. Of those that a mesh axis runs over, the one named last changes fastest.
Arguments:
- edge_feats: bfloat16 [4, 16384, 1280], P('rep', 'run'), may hold values from -6 to 6
- edge_grads: bfloat16 [4, 16384, 640], P('rep', 'run'), may hold values from -0.059814453 to 0.059814453
- edge_system: int32 [4, 16384], P('rep', 'run'), may hold values from 0 to 5, as said below
- edge_count: int32 [4, 8], P('rep', 'run'), may hold values from 1025 to 2048
- coef: float32 [4, 6, 32], P('rep'), may hold values from 0.05 to 1
- weights: float32 [32, 1280, 640], P('rep', 'run'), may hold values from -0.15625 to 0.15625
- first_moment: float32 [32, 1280, 640], P('rep', 'run'), may hold values from -6 to 6
- second_moment: float32 [32, 1280, 640], P('rep', 'run'), may hold values from 1 to 10
Outputs:
- new_weights: float32 [32, 1280, 640], P('rep', 'run')
- new_first: float32 [32, 1280, 640], P('rep', 'run')
- new_second: float32 [32, 1280, 640], P('rep', 'run')
- merged_next: bfloat16 [4, 6, 1280, 640], P('rep', None, 'run')
Inputs may be any that keep to these rules, and one draw needn't show every extreme that they name: `edge_system`: along each replica's rows the system never falls; every system number appears; the live rows of one device belong to one or two systems, two on some device in every draw.
All inputs are finite; a program needn't handle non-finite values.
Results may differ from a plain program's by a relative error of at most 0.001.
The roundings to bfloat16 on the way count: a program that leaves them out, or rounds other values in their place, can miss the bound.
Values may be sent and summed in bfloat16 or wider, within the bound.
A program may use at most 128 MiB of HBM per device.

v0:
```python
import functools
import jax
import jax.numpy as jnp
from jax import lax
from jax.experimental import pallas as pl
from jax.experimental.pallas import tpu as pltpu
from jax.sharding import PartitionSpec as P

MESH = pl.DeviceIdType.MESH
LANES = 128


def step_kernel(
    n_run, n_rep, nsys, held, chunks, chunk_rows, dout,
    slots, meta, coef_out, merge_coef, weights, moment1, moment2,
    weights_out, moment1_out, moment2_out, merged_out,
    land, meta_land, coef_land, sums, rounded, wbuf, fbuf, sbuf, mbuf,
    a2a_send, a2a_recv, meta_send, meta_recv, coef_send, coef_recv,
    x_send, x_recv, pair_send, pair_recv, own_sem, in_sem, out_sem,
):
    me = lax.axis_index("run")
    rep = lax.axis_index("rep")
    partner = rep + 1 - 2 * lax.rem(rep, 2)
    n_x = n_rep // 2
    experts = n_rep * held

    loads = [
        pltpu.make_async_copy(src, dst, in_sem.at[i])
        for i, (src, dst) in enumerate(((weights, wbuf), (moment1, fbuf), (moment2, sbuf)))
    ]
    for load in loads:
        load.start()
    own = pltpu.make_async_copy(slots.at[me], land.at[me], own_sem)
    own.start()

    barrier = pltpu.get_barrier_semaphore()
    for o in range(1, n_run):
        pl.semaphore_signal(
            barrier, inc=1, device_id={"run": lax.rem(me + o, n_run)}, device_id_type=MESH
        )
    for o in range(1, n_rep):
        pl.semaphore_signal(
            barrier, inc=1, device_id={"rep": lax.rem(rep + o, n_rep)}, device_id_type=MESH
        )
    pl.semaphore_wait(barrier, n_run + n_rep - 2)

    started = []

    def send(src, dst, send_sem, recv_sem, device):
        copy = pltpu.make_async_remote_copy(
            src_ref=src, dst_ref=dst, send_sem=send_sem, recv_sem=recv_sem,
            device_id=device, device_id_type=MESH,
        )
        copy.start()
        started.append(copy)
        return copy

    metas = [
        send(meta, meta_land.at[me], meta_send.at[o - 1], meta_recv.at[o - 1],
             {"run": lax.rem(me + o, n_run)})
        for o in range(1, n_run)
    ]
    coefs = []
    for o in range(1, n_rep):
        dest = lax.rem(rep + o, n_rep)
        coefs.append(
            send(coef_out.at[dest], coef_land.at[rep], coef_send.at[o - 1], coef_recv.at[o - 1],
                 {"rep": dest})
        )
    pieces = []

    def scatter(c):
        if c >= chunks:
            return
        pieces.append([])
        for o in range(1, n_run):
            dest = jnp.bitwise_xor(me, o)
            pieces[c].append(
                send(slots.at[dest, c], land.at[me, c], a2a_send.at[c, o - 1],
                     a2a_recv.at[c, o - 1], {"run": dest})
            )

    ahead = 1
    for c in range(ahead):
        scatter(c)

    meta_land[me] = meta[...]
    coef_land[rep] = coef_out[rep]
    own.wait()
    for copy in metas:
        copy.wait_recv()
    for copy in coefs:
        copy.wait_recv()
    for load in loads:
        load.wait()

    group = 16 if chunk_rows % 16 == 0 else chunk_rows
    lane_steps = dout // LANES

    def tiles(body):
        def step(i, carry):
            row = lax.div(i, lane_steps) * group
            lane = lax.rem(i, lane_steps) * LANES
            body(pl.multiple_of(row, group), pl.multiple_of(lane, LANES))
            return carry

        lax.fori_loop(0, (chunk_rows // group) * lane_steps, step, 0)

    def spread(buf, kind, c):
        direct = send(buf.at[c, rep], buf.at[c, rep], pair_send.at[kind, c, 0],
                      pair_recv.at[kind, c, 0], {"rep": partner})
        across = [
            send(buf.at[c, rep], buf.at[c, rep], x_send.at[kind, c, j - 1],
                 x_recv.at[kind, c, j - 1], {"rep": lax.rem(rep + 2 * j, n_rep)})
            for j in range(1, n_x)
        ]
        return direct, across

    def collect(buf, kind, c, direct, across):
        relays = []
        for j in range(1, n_x):
            across[j - 1].wait_recv()
            slot = lax.rem(rep + n_rep - 2 * j, n_rep)
            relays.append(
                send(buf.at[c, slot], buf.at[c, slot], pair_send.at[kind, c, j],
                     pair_recv.at[kind, c, j], {"rep": partner})
            )
        direct.wait_recv()
        for relay in relays:
            relay.wait_recv()

    def sum_systems(c):
        def body(row, lane):
            rows = pl.ds(row, group)
            total = [jnp.zeros((group, LANES), jnp.float32)] * nsys
            for k in range(n_run):
                low = land[k, c, rows, pl.ds(lane, LANES)].astype(jnp.float32)
                high = land[k, c, rows, pl.ds(lane + dout, LANES)].astype(jnp.float32)
                for s in range(nsys):
                    total[s] = (
                        total[s]
                        + meta_land[k, s + 1 : s + 2, :] * low
                        + meta_land[k, s : s + 1, :] * high
                    )
            for s in range(nsys):
                sums[c, rep, s, rows, pl.ds(lane, LANES)] = total[s].astype(jnp.bfloat16)

        tiles(body)

    def update(c):
        def body(row, lane):
            rows, lanes = pl.ds(row, group), pl.ds(lane, LANES)
            place = pl.ds(c * chunk_rows + row, group)
            grad = [jnp.zeros((group, LANES), jnp.float32)] * held
            for r in range(n_rep):
                for s in range(nsys):
                    part = sums[c, r, s, rows, lanes].astype(jnp.float32)
                    for e in range(held):
                        at = s * held + e
                        grad[e] = grad[e] + coef_land[r, at : at + 1, :] * part
            for e in range(held):
                new_first = 0.9 * fbuf[e, place, lanes] + 0.1 * grad[e]
                new_second = 0.999 * sbuf[e, place, lanes] + 0.001 * grad[e] * grad[e]
                corr_first = 1.0 - 0.9**10
                corr_second = 1.0 - 0.999**10
                new_weights = wbuf[e, place, lanes] - 0.01 * (new_first / corr_first) / (
                    jnp.sqrt(new_second / corr_second) + 1e-08
                )
                fbuf[e, place, lanes] = new_first
                sbuf[e, place, lanes] = new_second
                wbuf[e, place, lanes] = new_weights
                rounded[c, rep, e, rows, lanes] = new_weights.astype(jnp.bfloat16)

        tiles(body)

    def merge(c):
        def body(row, lane):
            rows, lanes = pl.ds(row, group), pl.ds(lane, LANES)
            total = [jnp.zeros((group, LANES), jnp.float32)] * nsys
            for r in range(n_rep):
                for e in range(held):
                    part = rounded[c, r, e, rows, lanes].astype(jnp.float32)
                    for s in range(nsys):
                        at = s * experts + r * held + e
                        total[s] = total[s] + merge_coef[at : at + 1, :] * part
            for s in range(nsys):
                mbuf[c, s, rows, lanes] = total[s].astype(jnp.bfloat16)

        tiles(body)

    stores = []

    def store(src, dst, kind, c):
        copy = pltpu.make_async_copy(src, dst, out_sem.at[kind, c])
        copy.start()
        stores.append(copy)

    def finish(c, moving):
        collect(rounded, 1, c, *moving)
        merge(c)
        store(mbuf.at[c], merged_out.at[:, pl.ds(c * chunk_rows, chunk_rows), :], 3, c)

    waiting = None
    for c in range(chunks):
        for copy in pieces[c]:
            copy.wait_recv()
        sum_systems(c)
        moving = spread(sums, 0, c)
        scatter(c + ahead)
        if waiting is not None:
            finish(c - 1, waiting)
        collect(sums, 0, c, *moving)
        update(c)
        waiting = spread(rounded, 1, c)
        place = pl.ds(c * chunk_rows, chunk_rows)
        store(wbuf.at[:, place, :], weights_out.at[:, place, :], 0, c)
        store(fbuf.at[:, place, :], moment1_out.at[:, place, :], 1, c)
        store(sbuf.at[:, place, :], moment2_out.at[:, place, :], 2, c)
    finish(chunks - 1, waiting)
    for copy in started:
        copy.wait_send()
    for copy in stores:
        copy.wait()


def on_device(
    n_run, n_rep,
    edge_feats, edge_grads, edge_system, edge_count, coef, weights, first_moment, second_moment
):
    feats = edge_feats[0]
    grads = edge_grads[0]
    system = edge_system[0]
    live_count = edge_count[0, 0]
    group_coef = coef[0]
    nsys, experts = group_coef.shape
    held, din_local, dout = weights.shape
    live = jnp.arange(system.shape[0]) < live_count
    first = system[0]
    empty = jnp.zeros_like(grads)
    lower = jnp.where((live & (system == first))[:, None], grads, empty)
    upper = jnp.where((live & (system == first + 1))[:, None], grads, empty)
    right = jnp.concatenate([lower, upper], axis=1)
    slots = lax.dot_general(
        feats, right, (((0,), (0,)), ((), ())), preferred_element_type=jnp.float32
    ).astype(jnp.bfloat16)

    chunk_rows = 32 if din_local % 32 == 0 else din_local
    chunks = din_local // chunk_rows
    slots = slots.reshape(n_run, chunks, chunk_rows, 2 * dout)
    meta_rows = -(-(nsys + 1) // 8) * 8
    marks = (jnp.arange(meta_rows) == first + 1).astype(jnp.float32)
    meta = jnp.broadcast_to(marks[:, None], (meta_rows, LANES))
    by_owner = group_coef.reshape(nsys, n_rep, held).transpose(1, 0, 2).reshape(n_rep, nsys * held)
    coef_out = jnp.broadcast_to(by_owner[:, :, None], (n_rep, nsys * held, LANES))
    merge_coef = jnp.broadcast_to(
        group_coef.reshape(nsys * experts)[:, None], (nsys * experts, LANES)
    )

    bf16, f32 = jnp.bfloat16, jnp.float32
    dma = pltpu.SemaphoreType.DMA
    n_x = n_rep // 2
    anywhere = pl.BlockSpec(memory_space=pl.ANY)
    vmem = pl.BlockSpec(memory_space=pltpu.VMEM)
    block = jax.ShapeDtypeStruct(weights.shape, f32)
    outs = pl.pallas_call(
        functools.partial(step_kernel, n_run, n_rep, nsys, held, chunks, chunk_rows, dout),
        out_shape=(block, block, block, jax.ShapeDtypeStruct((nsys, din_local, dout), bf16)),
        in_specs=[anywhere, vmem, vmem, vmem, anywhere, anywhere, anywhere],
        out_specs=(anywhere,) * 4,
        scratch_shapes=[
            pltpu.VMEM(slots.shape, bf16),
            pltpu.VMEM((n_run, meta_rows, LANES), f32),
            pltpu.VMEM(coef_out.shape, f32),
            pltpu.VMEM((chunks, n_rep, nsys, chunk_rows, dout), bf16),
            pltpu.VMEM((chunks, n_rep, held, chunk_rows, dout), bf16),
            pltpu.VMEM(weights.shape, f32),
            pltpu.VMEM(weights.shape, f32),
            pltpu.VMEM(weights.shape, f32),
            pltpu.VMEM((chunks, nsys, chunk_rows, dout), bf16),
            dma((chunks, n_run - 1)),
            dma((chunks, n_run - 1)),
            dma((n_run - 1,)),
            dma((n_run - 1,)),
            dma((n_rep - 1,)),
            dma((n_rep - 1,)),
            dma((2, chunks, n_x)),
            dma((2, chunks, n_x)),
            dma((2, chunks, n_x)),
            dma((2, chunks, n_x)),
            dma,
            dma((3,)),
            dma((4, chunks)),
        ],
        compiler_params=pltpu.CompilerParams(
            collective_id=0, has_side_effects=True, vmem_limit_bytes=56 * 1024 * 1024
        ),
        name="exchange_step",
    )(slots, meta, coef_out, merge_coef, weights, first_moment, second_moment)
    return (*outs[:3], outs[3][None])


def solution(mesh):
    placed = (
        P("rep", "run", None),
        P("rep", "run", None),
        P("rep", "run"),
        P("rep", "run"),
        P("rep", None, None),
        P("rep", "run", None),
        P("rep", "run", None),
        P("rep", "run", None),
    )
    return jax.shard_map(
        functools.partial(on_device, mesh.shape["run"], mesh.shape["rep"]),
        mesh=mesh,
        in_specs=placed,
        out_specs=(
            P("rep", "run", None),
            P("rep", "run", None),
            P("rep", "run", None),
            P("rep", None, "run", None),
        ),
        check_vma=False,
    )
```

profile of v0, /device:TPU:0, one launch (start us, length us, event | category | flops | bytes accessed | tf_op | source)
XLA Modules:
  0.0 144.4 jit_solution(9052423319386039900)
XLA Ops:
  1.3 1.2 slice.4
  3.1 1.4 compare_reduce_fusion.1
  4.5 0.7 broadcast_in_dim.44.meta
  5.2 0.7 reduce.2
  5.9 0.1 broadcast_in_dim.47
  6.0 0.1 reshape_squeeze.3
  6.0 0.1 broadcast_in_dim.45
  6.1 0.7 broadcast_in_dim.46.coef_out
  6.9 0.7 broadcast_in_dim.48.merge_coef
  7.6 0.0 copy-start.3
  7.6 3.7 %bitcast_select_fusion.1 = (bf16[2048,640]{1,0:T(8,128)(2,1)S(1)}, bf16[2048,640]{1,0:T(8,128)(2,1)S(1)}) fusion(bf16[1,2048,640]{2,1,0:T(8,128)(2,1)} %param.9, pred[2048]{0:T(1024)(128)(4,1)S(1)} %get-tuple-element.17, pred[2048]{0:T(1024)(128)(4,1)S(1)} %get-tuple-element.16), kind=kLoop, calls=%fused_computation.6 | loop fusion | flops 2621440 | bytes 7868416 | tf_op jit(solution)/shard_map/jit(_where)/select_n | solution.py:240
  11.3 0.0 copy-done.3
  11.3 8.5 %convolution_convert_fusion = bf16[1280,1280]{0,1:T(8,128)(2,1)} fusion(bf16[2048,640]{1,0:T(8,128)(2,1)S(1)} %get-tuple-element.15, bf16[2048,640]{1,0:T(8,128)(2,1)S(1)} %get-tuple-element.14, bf16[1,2048,1280]{2,1,0:T(8,128)(2,1)S(1)} %copy-done.3), kind=kOutput, calls=%fused_computation | convolution fusion | flops 6723010560 | bytes 13762560 | tf_op jit(solution)/shard_map/dot_general | solution.py:243
  19.9 114.1 %exchange_step.1 = (f32[8,160,640]{2,1,0:T(8,128)}, f32[8,160,640]{2,1,0:T(8,128)}, f32[8,160,640]{2,1,0:T(8,128)}, bf16[6,160,640]{2,1,0:T(8,128)(2,1)}) custom-call(bf16[8,5,32,1280]{3,2,1,0:T(8,128)(2,1)} %bitcast.16, f32[8,128]{1,0:T(8,128)} %broadcast_in_dim.44.meta, f32[4,48,128]{2,1,0:T(8,128)} %broadcast_in_dim.46.coef_out, ...), custom_call_target="tpu_custom_call" | custom-call | tf_op jit(solution)/shard_map/exchange_step/pallas_call | solution.py:265
  134.0 0.0 copy-start.1
  134.0 4.0 %copy.21 = f32[8,160,640]{2,1,0:T(8,128)} copy(f32[8,160,640]{2,1,0:T(8,128)} %get-tuple-element.22) | data formatting | bytes 6553600
  138.1 0.0 copy-done.1
  138.1 0.0 copy-start
  138.1 1.7 %copy.22 = f32[8,160,640]{2,1,0:T(8,128)} copy(f32[8,160,640]{2,1,0:T(8,128)S(1)} %copy-done.1) | data formatting | bytes 6553600
  139.8 1.4 copy-done
  141.2 0.0 copy-start.2
  141.2 1.7 %copy.23 = f32[8,160,640]{2,1,0:T(8,128)} copy(f32[8,160,640]{2,1,0:T(8,128)S(1)} %copy-done) | data formatting | bytes 6553600
  142.9 0.5 copy-done.2
  143.3 1.0 copy.24
  (3 shorter events, 0.0 us)
Async XLA Ops:
  7.6 3.7 %copy-start.3 = (bf16[1,2048,1280]{2,1,0:T(8,128)(2,1)S(1)}, bf16[1,2048,1280]{2,1,0:T(8,128)(2,1)}, u32[]{:S(2)}) copy-start(bf16[1,2048,1280]{2,1,0:T(8,128)(2,1)} %param.8) | copy-start | bytes 15728644
  134.0 4.0 %copy-start.1 = (f32[8,160,640]{2,1,0:T(8,128)S(1)}, f32[8,160,640]{2,1,0:T(8,128)}, u32[]{:S(2)}) copy-start(f32[8,160,640]{2,1,0:T(8,128)} %get-tuple-element.23) | copy-start | bytes 9830404
  138.1 3.1 %copy-start = (f32[8,160,640]{2,1,0:T(8,128)S(1)}, f32[8,160,640]{2,1,0:T(8,128)}, u32[]{:S(2)}) copy-start(f32[8,160,640]{2,1,0:T(8,128)} %get-tuple-element.24) | copy-start | bytes 9830404
  141.2 2.2 %copy-start.2 = (bf16[6,160,640]{2,1,0:T(8,128)(2,1)S(1)}, bf16[6,160,640]{2,1,0:T(8,128)(2,1)}, u32[]{:S(2)}) copy-start(bf16[6,160,640]{2,1,0:T(8,128)(2,1)} %get-tuple-element.11) | copy-start | bytes 3686404
where the time goes:
time: 145 us; the launch traced here: 144 us
  Pallas kernels  114 us (79%)
  local copies, waits for them, and re-layouts  13.9 us (10%)
  matrix products  8.53 us (6%)
  other arithmetic  5.83 us (4%)
  between operations  1.99 us (1%)
    pallas_call x1, Pallas kernels, on_device(): pl.pallas_call(functools.partial(step_kernel, n_run, n_rep, nsys, held, c...  114 us
    unnamed x12, local copies, waits for them, and re-layouts  10.3 us
    dot_general x1, matrix products, on_device(): lax.dot_general(feats, right, (((0,), (0,)), ((), ())), preferred_element...  8.53 us
    select_n x1, other arithmetic, on_device(): lower = jnp.where((live & (system == first))[:, None], grads, empty)  3.72 us

commit v1 on v0

v1 whole, which is shorter than its diff:
```python
import functools
import jax
import jax.numpy as jnp
from jax import lax
from jax.experimental import pallas as pl
from jax.experimental.pallas import tpu as pltpu
from jax.sharding import PartitionSpec as P

MESH = pl.DeviceIdType.MESH
LANES = 128
DEPTH = 256
AHEAD = 2


def step_kernel(
    n_run, n_rep, nsys, held, units, hr, per_block,
    coef, count, system, feats, grads, weights, moment1, moment2,
    wbuf, fbuf, sbuf, mbuf,
    fin, fturn, gin, gpair, out_slots, land, sums, rounded,
    mark, mark_land, coef_mine, coef_land,
    edge_sem, in_sem, own_sem, a2a_send, a2a_recv, mark_send, mark_recv,
    coef_send, coef_recv, x_send, x_recv, pair_send, pair_recv,
):
    me = lax.axis_index("run")
    rep = lax.axis_index("rep")
    partner = rep + 1 - 2 * lax.rem(rep, 2)
    n_x = n_rep // 2
    n_edge, din = fin.shape
    steps = n_edge // DEPTH
    local = din // n_run
    splits = local // hr
    n_units = len(units)
    f32, bf16 = jnp.float32, jnp.bfloat16

    barrier = pltpu.get_barrier_semaphore()
    for o in range(1, n_run):
        pl.semaphore_signal(
            barrier, inc=1, device_id={"run": jnp.bitwise_xor(me, o)}, device_id_type=MESH
        )
    for o in range(1, n_rep):
        pl.semaphore_signal(
            barrier, inc=1, device_id={"rep": lax.rem(rep + o, n_rep)}, device_id_type=MESH
        )

    edge_loads = []
    for k in range(steps):
        rows = pl.ds(k * DEPTH, DEPTH)
        pair = (
            pltpu.make_async_copy(feats.at[0, rows], fin.at[rows], edge_sem.at[0, k]),
            pltpu.make_async_copy(grads.at[0, rows], gin.at[rows], edge_sem.at[1, k]),
        )
        for copy in pair:
            copy.start()
        edge_loads.append(pair)
    loads = [
        pltpu.make_async_copy(src, dst, in_sem.at[i])
        for i, (src, dst) in enumerate(((weights, wbuf), (moment1, fbuf), (moment2, sbuf)))
    ]
    for load in loads:
        load.start()

    ids = system[...]
    first = jnp.min(ids, axis=1, keepdims=True)
    live = lax.broadcasted_iota(jnp.int32, ids.shape, 1) < count[0, 0]
    split = jnp.sum((live & (ids == first)).astype(jnp.int32), axis=1, keepdims=True)
    end = jnp.sum((live & (ids <= first + 1)).astype(jnp.int32), axis=1, keepdims=True)
    at = lax.broadcasted_iota(jnp.int32, mark.shape, 0)
    mark[...] = (at == first + 1).astype(f32)

    def spell(i, carry):
        r = lax.div(i, nsys * held)
        j = lax.rem(i, nsys * held)
        value = coef[0, lax.div(j, held), r * held + lax.rem(j, held)]
        coef_mine[r, pl.ds(j, 1), :] = jnp.full((1, LANES), value, f32)
        return carry

    lax.fori_loop(0, n_rep * nsys * held, spell, 0)

    started = []

    def send(src, dst, send_sem, recv_sem, device):
        copy = pltpu.make_async_remote_copy(
            src_ref=src, dst_ref=dst, send_sem=send_sem, recv_sem=recv_sem,
            device_id=device, device_id_type=MESH,
        )
        copy.start()
        started.append(copy)
        return copy

    def mask(c):
        for k in range(steps):
            rows = pl.ds(k * DEPTH, DEPTH)
            if c == 0:
                for copy in edge_loads[k]:
                    copy.wait()
                fturn[:, k * DEPTH : (k + 1) * DEPTH] = fin[rows, :].T
            part = gin[rows, c * LANES : (c + 1) * LANES].astype(f32)
            place = lax.broadcasted_iota(jnp.int32, part.shape, 0) + k * DEPTH
            low = jnp.where(place < split, part, 0.0)
            high = jnp.where((place >= split) & (place < end), part, 0.0)
            gpair[rows, :LANES] = low.astype(bf16)
            gpair[rows, LANES:] = high.astype(bf16)

    def multiply(c):
        size = per_block * local

        def step(i, carry):
            base = pl.multiple_of(i * size, size)
            block = jnp.dot(
                fturn[pl.ds(base, size), :], gpair[...], preferred_element_type=f32
            )
            for p in range(per_block):
                for h in range(splits):
                    rows = slice(p * local + h * hr, p * local + (h + 1) * hr)
                    u = c * splits + h
                    owner = i * per_block + p
                    out_slots[u, owner, 0] = block[rows, :LANES].astype(bf16)
                    out_slots[u, owner, 1] = block[rows, LANES:].astype(bf16)
            return carry

        lax.fori_loop(0, n_run // per_block, step, 0)

    pieces = []

    def scatter(u):
        own = pltpu.make_async_copy(out_slots.at[u, me], land.at[u, me], own_sem.at[u])
        own.start()
        pieces.append([own])
        for o in range(1, n_run):
            dest = jnp.bitwise_xor(me, o)
            pieces[u].append(
                send(out_slots.at[u, dest], land.at[u, me], a2a_send.at[u, o - 1],
                     a2a_recv.at[u, o - 1], {"run": dest})
            )

    marks, coefs = [], []
    mask(0)
    multiply(0)
    pl.semaphore_wait(barrier, n_run + n_rep - 2)
    for o in range(1, n_run):
        marks.append(
            send(mark, mark_land.at[me], mark_send.at[o - 1], mark_recv.at[o - 1],
                 {"run": jnp.bitwise_xor(me, o)})
        )
    for o in range(1, n_rep):
        dest = lax.rem(rep + o, n_rep)
        coefs.append(
            send(coef_mine.at[dest], coef_land.at[rep], coef_send.at[o - 1],
                 coef_recv.at[o - 1], {"rep": dest})
        )
    for u in range(splits):
        scatter(u)
    if n_units > splits:
        mask(1)
        multiply(1)
    for u in range(splits, AHEAD):
        scatter(u)

    mark_land[me] = mark[...]
    coef_land[rep] = coef_mine[rep]

    group = 16 if hr % 16 == 0 else hr

    def tiles(body):
        def step(i, carry):
            body(pl.multiple_of(i * group, group))
            return carry

        lax.fori_loop(0, hr // group, step, 0)

    def spread(buf, kind, u):
        direct = send(buf.at[u, rep], buf.at[u, rep], pair_send.at[kind, u, 0],
                      pair_recv.at[kind, u, 0], {"rep": partner})
        across = [
            send(buf.at[u, rep], buf.at[u, rep], x_send.at[kind, u, j - 1],
                 x_recv.at[kind, u, j - 1], {"rep": lax.rem(rep + 2 * j, n_rep)})
            for j in range(1, n_x)
        ]
        return [direct], across

    def relay(buf, kind, u, moving):
        near, across = moving
        for j in range(1, n_x):
            across[j - 1].wait_recv()
            slot = lax.rem(rep + n_rep - 2 * j, n_rep)
            near.append(
                send(buf.at[u, slot], buf.at[u, slot], pair_send.at[kind, u, j],
                     pair_recv.at[kind, u, j], {"rep": partner})
            )

    def collect(moving):
        for copy in moving[0]:
            copy.wait_recv()

    def sum_systems(u):
        def body(row):
            rows = pl.ds(row, group)
            total = [jnp.zeros((group, LANES), f32)] * nsys
            for k in range(n_run):
                low = land[u, k, 0, rows, :].astype(f32)
                high = land[u, k, 1, rows, :].astype(f32)
                for s in range(nsys):
                    total[s] = (
                        total[s]
                        + mark_land[k, s + 1 : s + 2, :] * low
                        + mark_land[k, s : s + 1, :] * high
                    )
            for s in range(nsys):
                sums[u, rep, s, rows, :] = total[s].astype(bf16)

        tiles(body)

    def update(u):
        base, lane = units[u]

        def body(row):
            rows, lanes = pl.ds(row, group), slice(lane, lane + LANES)
            place = pl.ds(pl.multiple_of(base + row, 8), group)
            grad = [jnp.zeros((group, LANES), f32)] * held
            for r in range(n_rep):
                for s in range(nsys):
                    part = sums[u, r, s, rows, :].astype(f32)
                    for e in range(held):
                        at = s * held + e
                        grad[e] = grad[e] + coef_land[r, at : at + 1, :] * part
            for e in range(held):
                new_first = 0.9 * fbuf[e, place, lanes] + 0.1 * grad[e]
                new_second = 0.999 * sbuf[e, place, lanes] + 0.001 * grad[e] * grad[e]
                corr_first = 1.0 - 0.9**10
                corr_second = 1.0 - 0.999**10
                new_weights = wbuf[e, place, lanes] - (0.01 / corr_first) * new_first / (
                    jnp.sqrt(new_second * (1.0 / corr_second)) + 1e-08
                )
                fbuf[e, place, lanes] = new_first
                sbuf[e, place, lanes] = new_second
                wbuf[e, place, lanes] = new_weights
                rounded[u, rep, e, rows, :] = new_weights.astype(bf16)

        tiles(body)

    def merge(u):
        base, lane = units[u]

        def body(row):
            rows = pl.ds(row, group)
            place = pl.ds(pl.multiple_of(base + row, group), group)
            total = [jnp.zeros((group, LANES), f32)] * nsys
            for r in range(n_rep):
                for e in range(held):
                    part = rounded[u, r, e, rows, :].astype(f32)
                    for s in range(nsys):
                        at = s * held + e
                        total[s] = total[s] + coef_mine[r, at : at + 1, :] * part
            for s in range(nsys):
                mbuf[s, place, lane : lane + LANES] = total[s].astype(bf16)

        tiles(body)

    for copy in marks:
        copy.wait_recv()
    for copy in coefs:
        copy.wait_recv()
    for load in loads:
        load.wait()

    moved_sums, moved_new = {}, {}
    for t in range(n_units + 2):
        if t < n_units:
            pieces[t][0].wait()
            for copy in pieces[t][1:]:
                copy.wait_recv()
        if t + AHEAD < n_units:
            scatter(t + AHEAD)
        if 1 <= t <= n_units:
            relay(sums, 0, t - 1, moved_sums[t - 1])
        if t < n_units:
            sum_systems(t)
            moved_sums[t] = spread(sums, 0, t)
        if t >= 2:
            relay(rounded, 1, t - 2, moved_new[t - 2])
        if 1 <= t <= n_units:
            collect(moved_sums[t - 1])
            update(t - 1)
            moved_new[t - 1] = spread(rounded, 1, t - 1)
        if t >= 2:
            collect(moved_new[t - 2])
            merge(t - 2)
        c = t // splits + 2
        if t % splits == 0 and c * splits < n_units:
            mask(c)
            multiply(c)
    for copy in started:
        copy.wait_send()


def store_kernel(w, f, s, m, w_out, f_out, s_out, m_out, sems):
    copies = [
        pltpu.make_async_copy(src, dst, sems.at[i])
        for i, (src, dst) in enumerate(((w, w_out), (f, f_out), (s, s_out), (m, m_out.at[0])))
    ]
    for copy in copies:
        copy.start()
    for copy in copies:
        copy.wait()


def on_device(
    n_run, n_rep,
    edge_feats, edge_grads, edge_system, edge_count, coef, weights, first_moment, second_moment
):
    _, nsys, experts = coef.shape
    held, local, dout = weights.shape
    _, n_edge, din = edge_feats.shape
    hr = local // 2 if local % 32 == 0 else local
    units = [(row, lane) for lane in range(0, dout, LANES) for row in range(0, local, hr)]
    n_units = len(units)
    per_block = 1
    while per_block * local % 16:
        per_block *= 2

    bf16, f32 = jnp.bfloat16, jnp.float32
    dma = pltpu.SemaphoreType.DMA
    n_x = n_rep // 2
    mark_rows = -(-(nsys + 1) // 8) * 8
    anywhere = pl.BlockSpec(memory_space=pl.ANY)
    vmem = pl.BlockSpec(memory_space=pltpu.VMEM)
    smem = pl.BlockSpec(memory_space=pltpu.SMEM)
    kept = pltpu.VMEM(weights.shape, f32)
    outs = pl.pallas_call(
        functools.partial(step_kernel, n_run, n_rep, nsys, held, units, hr, per_block),
        out_shape=(kept, kept, kept, pltpu.VMEM((nsys, local, dout), bf16)),
        in_specs=[smem, smem, vmem] + [anywhere] * 5,
        out_specs=(vmem,) * 4,
        scratch_shapes=[
            pltpu.VMEM((n_edge, din), bf16),
            pltpu.VMEM((din, n_edge), bf16),
            pltpu.VMEM((n_edge, dout), bf16),
            pltpu.VMEM((n_edge, 2 * LANES), bf16),
            pltpu.VMEM((n_units, n_run, 2, hr, LANES), bf16),
            pltpu.VMEM((n_units, n_run, 2, hr, LANES), bf16),
            pltpu.VMEM((n_units, n_rep, nsys, hr, LANES), bf16),
            pltpu.VMEM((n_units, n_rep, held, hr, LANES), bf16),
            pltpu.VMEM((mark_rows, LANES), f32),
            pltpu.VMEM((n_run, mark_rows, LANES), f32),
            pltpu.VMEM((n_rep, nsys * held, LANES), f32),
            pltpu.VMEM((n_rep, nsys * held, LANES), f32),
            dma((2, n_edge // DEPTH)),
            dma((3,)),
            dma((n_units,)),
            dma((n_units, n_run - 1)),
            dma((n_units, n_run - 1)),
            dma((n_run - 1,)),
            dma((n_run - 1,)),
            dma((n_rep - 1,)),
            dma((n_rep - 1,)),
            dma((2, n_units, n_x)),
            dma((2, n_units, n_x)),
            dma((2, n_units, n_x)),
            dma((2, n_units, n_x)),
        ],
        compiler_params=pltpu.CompilerParams(
            collective_id=0, has_side_effects=True, vmem_limit_bytes=46 * 1024 * 1024
        ),
        name="exchange_step",
    )(coef, edge_count, edge_system, edge_feats, edge_grads, weights, first_moment, second_moment)
    block = jax.ShapeDtypeStruct(weights.shape, f32)
    return pl.pallas_call(
        store_kernel,
        out_shape=(block, block, block, jax.ShapeDtypeStruct((1, nsys, local, dout), bf16)),
        in_specs=[vmem] * 4,
        out_specs=(anywhere,) * 4,
        scratch_shapes=[dma((4,))],
        compiler_params=pltpu.CompilerParams(vmem_limit_bytes=1024 * 1024),
        name="store",
    )(*(pltpu.with_memory_space_constraint(out, pltpu.VMEM) for out in outs))


def solution(mesh):
    placed = (
        P("rep", "run", None),
        P("rep", "run", None),
        P("rep", "run"),
        P("rep", "run"),
        P("rep", None, None),
        P("rep", "run", None),
        P("rep", "run", None),
        P("rep", "run", None),
    )
    return jax.shard_map(
        functools.partial(on_device, mesh.shape["run"], mesh.shape["rep"]),
        mesh=mesh,
        in_specs=placed,
        out_specs=(
            P("rep", "run", None),
            P("rep", "run", None),
            P("rep", "run", None),
            P("rep", None, "run", None),
        ),
        check_vma=False,
    )
```

time: 145 us -> 113 us (0.78)
  local copies, waits for them, and re-layouts: 13.9 us -> 1.28 us
  matrix products: 8.53 us -> 0 us
  other arithmetic: 5.83 us -> 0 us
  Pallas kernels: 114 us -> 110 us
    unnamed x12 -> x1, local copies, waits for them, and re-layouts: 10.3 us -> 1.28 us
    dot_general x1 -> x0, matrix products: 8.53 us -> none  [on_device(): lax.dot_general(feats, right, (((0,), (0,)), ((), ())), preferred_element...]
    pallas_call x1 -> x2, Pallas kernels: 114 us -> 110 us  [the longest x1 105 us: on_device(): pl.pallas_call(functools.partial(step_kernel, n_run, n_rep, nsys, held, u...]
    select_n x1 -> x0, other arithmetic: 3.72 us -> none  [on_device(): lower = jnp.where((live & (system == first))[:, None], grads, empty)]
    broadcast_in_dim x5 -> x0, local copies, waits for them, and re-layouts: 2.29 us -> none  [the longest x2 0.82 us: on_device(): jnp.broadcast_to(by_owner[:, :, None], (n_rep, nsys * held, LANES))]
where the time goes in v1:
time: 113 us; the launch traced here: 112 us
  Pallas kernels  110 us (97%)
  between operations  1.29 us (1%)
  local copies, waits for them, and re-layouts  1.28 us (1%)
    pallas_call x1, Pallas kernels, on_device(): pl.pallas_call(functools.partial(step_kernel, n_run, n_rep, nsys, held, u...  105 us
    pallas_call x1, Pallas kernels, on_device(): pl.pallas_call(store_kernel, out_shape=(block, block, block, jax.ShapeDty...  4.21 us

profile of v1, /device:TPU:0, one launch (start us, length us, event | category | flops | bytes accessed | tf_op | source)
XLA Modules:
  0.0 112.2 jit_solution(11369140878916155677)
XLA Ops:
  1.3 1.3 %copy.12.coef = f32[1,6,32]{2,1,0:T(8,128)} copy(f32[1,6,32]{2,0,1:T(1,128)} %param.12) | data formatting | bytes 1536 | tf_op args[4]
  2.6 105.4 %exchange_step.1 = (f32[8,160,640]{2,1,0:T(8,128)S(1)}, f32[8,160,640]{2,1,0:T(8,128)S(1)}, f32[8,160,640]{2,1,0:T(8,128)S(1)}, bf16[6,160,640]{2,1,0:T(8,128)(2,1)S(1)}) custom-call(f32[1,6,32]{2,1,0:T(8,128)} %copy.12.coef, s32[1,1]{1,0:T(1,128)S(6)} %copy.13.count, s32[1,2048]{1,0:T(1,128)} %system.1, bf16[1,2048,1280]{2,1,0:T(8,128)(2,1)} %feats.1, ...), custom_call_target="tpu_custom_call" | custom-call | tf_op jit(solution)/shard_map/exchange_step/pallas_call | solution.py:329
  108.0 4.2 %store.1 = (f32[8,160,640]{2,1,0:T(8,128)}, f32[8,160,640]{2,1,0:T(8,128)}, f32[8,160,640]{2,1,0:T(8,128)}, bf16[1,6,160,640]{3,2,1,0:T(8,128)(2,1)}) custom-call(f32[8,160,640]{2,1,0:T(8,128)S(1)} %get-tuple-element.8.w, f32[8,160,640]{2,1,0:T(8,128)S(1)} %get-tuple-element.9.f, f32[8,160,640]{2,1,0:T(8,128)S(1)} %get-tuple-element.10.s, ...), custom_call_target="tpu_custom_call" | custom-call | tf_op jit(solution)/shard_map/store/pallas_call | solution.py:367

commit v2 on v1

v2 whole, which is shorter than its diff:
```python
import functools
import jax
import jax.numpy as jnp
from jax import lax
from jax.experimental import pallas as pl
from jax.experimental.pallas import tpu as pltpu
from jax.sharding import PartitionSpec as P

MESH = pl.DeviceIdType.MESH
LANES = 128
DEPTH = 256


def step_kernel(
    n_run, n_rep, nsys, held, units, bands,
    coef, count, system, feats, grads, weights, moment1, moment2,
    wbuf, fbuf, sbuf, mbuf,
    fin, fturn, gin, gpair, out_slots, land, sums, rounded,
    mark, mark_land, coef_mine, coef_land,
    edge_sem, in_sem, own_sem, a2a_send, a2a_recv, mark_send, mark_recv,
    coef_send, coef_recv, x_send, x_recv, pair_send, pair_recv,
):
    me = lax.axis_index("run")
    rep = lax.axis_index("rep")
    partner = rep + 1 - 2 * lax.rem(rep, 2)
    n_x = n_rep // 2
    n_edge, din = fin.shape
    steps = n_edge // DEPTH
    local = din // n_run
    n_units = len(units)
    f32, bf16 = jnp.float32, jnp.bfloat16

    barrier = pltpu.get_barrier_semaphore()
    for o in range(1, n_run):
        pl.semaphore_signal(
            barrier, inc=1, device_id={"run": jnp.bitwise_xor(me, o)}, device_id_type=MESH
        )
    for o in range(1, n_rep):
        pl.semaphore_signal(
            barrier, inc=1, device_id={"rep": lax.rem(rep + o, n_rep)}, device_id_type=MESH
        )

    edge_loads = []
    for k in range(steps):
        rows = pl.ds(k * DEPTH, DEPTH)
        pair = (
            pltpu.make_async_copy(feats.at[0, rows], fin.at[rows], edge_sem.at[0, k]),
            pltpu.make_async_copy(grads.at[0, rows], gin.at[rows], edge_sem.at[1, k]),
        )
        for copy in pair:
            copy.start()
        edge_loads.append(pair)
    loads = [
        pltpu.make_async_copy(src, dst, in_sem.at[i])
        for i, (src, dst) in enumerate(((weights, wbuf), (moment1, fbuf), (moment2, sbuf)))
    ]

    ids = system[...]
    first = jnp.min(ids, axis=1, keepdims=True)
    live = lax.broadcasted_iota(jnp.int32, ids.shape, 1) < count[0, 0]
    split = jnp.sum((live & (ids == first)).astype(jnp.int32), axis=1, keepdims=True)
    end = jnp.sum((live & (ids <= first + 1)).astype(jnp.int32), axis=1, keepdims=True)
    at = lax.broadcasted_iota(jnp.int32, mark.shape, 0)
    mark[...] = (at == first + 1).astype(f32)

    def spell(i, carry):
        r = lax.div(i, nsys * held)
        j = lax.rem(i, nsys * held)
        value = coef[lax.div(j, held), 0, r * held + lax.rem(j, held)]
        coef_mine[r, pl.ds(j, 1), :] = jnp.full((1, LANES), value, f32)
        return carry

    lax.fori_loop(0, n_rep * nsys * held, spell, 0)

    started = []

    def send(src, dst, send_sem, recv_sem, device):
        copy = pltpu.make_async_remote_copy(
            src_ref=src, dst_ref=dst, send_sem=send_sem, recv_sem=recv_sem,
            device_id=device, device_id_type=MESH,
        )
        copy.start()
        started.append(copy)
        return copy

    def mask(c):
        for k in range(steps):
            rows = pl.ds(k * DEPTH, DEPTH)
            if c == 0:
                for copy in edge_loads[k]:
                    copy.wait()
                turned = fin[rows, :].T
                for at, size in bands:
                    for owner in range(n_run):
                        row = n_run * at + owner * size
                        fturn[row : row + size, k * DEPTH : (k + 1) * DEPTH] = turned[
                            owner * local + at : owner * local + at + size
                        ]
            part = gin[rows, c * LANES : (c + 1) * LANES].astype(f32)
            place = lax.broadcasted_iota(jnp.int32, part.shape, 0) + k * DEPTH
            low = jnp.where(place < split, part, 0.0)
            high = jnp.where((place >= split) & (place < end), part, 0.0)
            gpair[rows, :LANES] = low.astype(bf16)
            gpair[rows, LANES:] = high.astype(bf16)

    def multiply(c, at, size):
        block = jnp.dot(
            fturn[n_run * at : n_run * (at + size), :], gpair[...], preferred_element_type=f32
        )
        for owner in range(n_run):
            rows = slice(owner * size, (owner + 1) * size)
            out_slots[c, owner, 0, at : at + size] = block[rows, :LANES].astype(bf16)
            out_slots[c, owner, 1, at : at + size] = block[rows, LANES:].astype(bf16)

    pieces = []

    def part_of(buf, u, *at):
        c, row, size = units[u]
        return buf.at[(c, *at, slice(None), pl.ds(row, size))]

    def scatter(u):
        own = pltpu.make_async_copy(
            part_of(out_slots, u, me), part_of(land, u, me), own_sem.at[u]
        )
        own.start()
        pieces.append([own])
        for o in range(n_run - 1, 0, -1):
            dest = jnp.bitwise_xor(me, o)
            pieces[u].append(
                send(part_of(out_slots, u, dest), part_of(land, u, me), a2a_send.at[u, o - 1],
                     a2a_recv.at[u, o - 1], {"run": dest})
            )

    masked, done = set(), set()

    def prepare(u):
        if u in done:
            return
        done.add(u)
        c, row, size = units[u]
        if c not in masked:
            masked.add(c)
            mask(c)
        for at, rows in bands:
            if row <= at < row + size:
                multiply(c, at, rows)

    ends = [c * local + row + size for c, row, size in units]

    def due(t):
        if t >= n_units:
            return []
        reach = (ends[t] if t >= 0 else 0) + local // 2
        return [u for u in range(len(pieces), n_units) if ends[u] - units[u][2] < reach]

    marks, coefs = [], []
    prepare(0)
    for load in loads:
        load.start()
    pl.semaphore_wait(barrier, n_run + n_rep - 2)
    for o in range(1, n_run):
        marks.append(
            send(mark, mark_land.at[me], mark_send.at[o - 1], mark_recv.at[o - 1],
                 {"run": jnp.bitwise_xor(me, o)})
        )
    for o in range(1, n_rep):
        dest = lax.rem(rep + o, n_rep)
        coefs.append(
            send(coef_mine.at[dest], coef_land.at[rep], coef_send.at[o - 1],
                 coef_recv.at[o - 1], {"rep": dest})
        )
    for u in due(-1):
        prepare(u)
        scatter(u)
    for u in due(0):
        prepare(u)

    mark_land[me] = mark[...]
    coef_land[rep] = coef_mine[rep]

    def tiles(u, body):
        _, base, size = units[u]
        group = 16 if size % 16 == 0 else size
        align = 16 if size % 16 == 0 else 8

        def step(i, carry):
            body(pl.ds(pl.multiple_of(base + i * group, align), group), (group, LANES))
            return carry

        lax.fori_loop(0, size // group, step, 0)

    def spread(buf, kind, u):
        direct = send(part_of(buf, u, rep), part_of(buf, u, rep), pair_send.at[kind, u, 0],
                      pair_recv.at[kind, u, 0], {"rep": partner})
        across = [
            send(part_of(buf, u, rep), part_of(buf, u, rep), x_send.at[kind, u, j - 1],
                 x_recv.at[kind, u, j - 1], {"rep": lax.rem(rep + 2 * j, n_rep)})
            for j in range(1, n_x)
        ]
        return [direct], across

    def relay(buf, kind, u, moving):
        near, across = moving
        for j in range(1, n_x):
            across[j - 1].wait_recv()
            slot = lax.rem(rep + n_rep - 2 * j, n_rep)
            near.append(
                send(part_of(buf, u, slot), part_of(buf, u, slot), pair_send.at[kind, u, j],
                     pair_recv.at[kind, u, j], {"rep": partner})
            )

    def collect(moving):
        for copy in moving[0]:
            copy.wait_recv()

    def sum_systems(u):
        c = units[u][0]

        def body(rows, shape):
            total = [jnp.zeros(shape, f32)] * nsys
            for k in range(n_run):
                low = land[c, k, 0, rows, :].astype(f32)
                high = land[c, k, 1, rows, :].astype(f32)
                for s in range(nsys):
                    total[s] = (
                        total[s]
                        + mark_land[k, s + 1 : s + 2, :] * low
                        + mark_land[k, s : s + 1, :] * high
                    )
            for s in range(nsys):
                sums[c, rep, s, rows, :] = total[s].astype(bf16)

        tiles(u, body)

    def update(u):
        c = units[u][0]
        lanes = slice(c * LANES, (c + 1) * LANES)

        def body(rows, shape):
            grad = [jnp.zeros(shape, f32)] * held
            for r in range(n_rep):
                for s in range(nsys):
                    part = sums[c, r, s, rows, :].astype(f32)
                    for e in range(held):
                        at = s * held + e
                        grad[e] = grad[e] + coef_land[r, at : at + 1, :] * part
            for e in range(held):
                new_first = 0.9 * fbuf[e, rows, lanes] + 0.1 * grad[e]
                new_second = 0.999 * sbuf[e, rows, lanes] + 0.001 * grad[e] * grad[e]
                corr_first = 1.0 - 0.9**10
                corr_second = 1.0 - 0.999**10
                new_weights = wbuf[e, rows, lanes] - (0.01 / corr_first) * new_first / (
                    jnp.sqrt(new_second * (1.0 / corr_second)) + 1e-08
                )
                fbuf[e, rows, lanes] = new_first
                sbuf[e, rows, lanes] = new_second
                wbuf[e, rows, lanes] = new_weights
                rounded[c, rep, e, rows, :] = new_weights.astype(bf16)

        tiles(u, body)

    def merge(u):
        c = units[u][0]
        lanes = slice(c * LANES, (c + 1) * LANES)

        def body(rows, shape):
            total = [jnp.zeros(shape, f32)] * nsys
            for r in range(n_rep):
                for e in range(held):
                    part = rounded[c, r, e, rows, :].astype(f32)
                    for s in range(nsys):
                        at = s * held + e
                        total[s] = total[s] + coef_mine[r, at : at + 1, :] * part
            for s in range(nsys):
                mbuf[s, rows, lanes] = total[s].astype(bf16)

        tiles(u, body)

    for copy in marks:
        copy.wait_recv()
    for copy in coefs:
        copy.wait_recv()

    moved_sums, moved_new = {}, {}
    for t in range(n_units + 3):
        if t < n_units:
            pieces[t][0].wait()
            for copy in pieces[t][1:]:
                copy.wait_recv()
        for u in due(t):
            scatter(u)
        if 1 <= t <= n_units:
            relay(sums, 0, t - 1, moved_sums[t - 1])
        if t < n_units:
            sum_systems(t)
            moved_sums[t] = spread(sums, 0, t)
        if 1 <= t <= n_units:
            collect(moved_sums[t - 1])
            if t == 1:
                for load in loads:
                    load.wait()
            update(t - 1)
            moved_new[t - 1] = spread(rounded, 1, t - 1)
        if 2 <= t <= n_units + 1:
            relay(rounded, 1, t - 2, moved_new[t - 2])
        if t >= 3:
            collect(moved_new[t - 3])
            merge(t - 3)
        for u in due(t + 1):
            prepare(u)
    for copy in started:
        copy.wait_send()


def store_kernel(w, f, s, m, w_out, f_out, s_out, m_out, sems):
    copies = [
        pltpu.make_async_copy(src, dst, sems.at[i])
        for i, (src, dst) in enumerate(((w, w_out), (f, f_out), (s, s_out), (m, m_out.at[0])))
    ]
    for copy in copies:
        copy.start()
    for copy in copies:
        copy.wait()


def pieces_of(rows):
    if rows % 32 or rows < 128:
        return ([(0, rows)],) * 3
    half = rows // 2
    step = half // 32 * 16
    usual = [(0, half), (half, half)]
    first = [(0, step), (step, half - step), (half, half)]
    last = [(0, half), (half, half - step), (rows - step, step)]
    return first, usual, usual


def on_device(
    n_run, n_rep,
    edge_feats, edge_grads, edge_system, edge_count, coef, weights, first_moment, second_moment
):
    _, nsys, experts = coef.shape
    held, local, dout = weights.shape
    _, n_edge, din = edge_feats.shape
    chunks = dout // LANES
    first, usual, last = pieces_of(local)
    plans = [first] + [usual] * (chunks - 2) + [last]
    units = [(c, row, size) for c in range(chunks) for row, size in plans[c]]
    cuts = sorted({row for plan in plans for row, _ in plan} | {local})
    bands = [(a, b - a) for a, b in zip(cuts, cuts[1:])]
    n_units = len(units)

    bf16, f32 = jnp.bfloat16, jnp.float32
    dma = pltpu.SemaphoreType.DMA
    n_x = n_rep // 2
    mark_rows = -(-(nsys + 1) // 8) * 8
    anywhere = pl.BlockSpec(memory_space=pl.ANY)
    vmem = pl.BlockSpec(memory_space=pltpu.VMEM)
    smem = pl.BlockSpec(memory_space=pltpu.SMEM)
    kept = pltpu.VMEM(weights.shape, f32)
    outs = pl.pallas_call(
        functools.partial(step_kernel, n_run, n_rep, nsys, held, units, bands),
        out_shape=(kept, kept, kept, pltpu.VMEM((nsys, local, dout), bf16)),
        in_specs=[smem, smem, vmem] + [anywhere] * 5,
        out_specs=(vmem,) * 4,
        scratch_shapes=[
            pltpu.VMEM((n_edge, din), bf16),
            pltpu.VMEM((din, n_edge), bf16),
            pltpu.VMEM((n_edge, dout), bf16),
            pltpu.VMEM((n_edge, 2 * LANES), bf16),
            pltpu.VMEM((chunks, n_run, 2, local, LANES), bf16),
            pltpu.VMEM((chunks, n_run, 2, local, LANES), bf16),
            pltpu.VMEM((chunks, n_rep, nsys, local, LANES), bf16),
            pltpu.VMEM((chunks, n_rep, held, local, LANES), bf16),
            pltpu.VMEM((mark_rows, LANES), f32),
            pltpu.VMEM((n_run, mark_rows, LANES), f32),
            pltpu.VMEM((n_rep, nsys * held, LANES), f32),
            pltpu.VMEM((n_rep, nsys * held, LANES), f32),
            dma((2, n_edge // DEPTH)),
            dma((3,)),
            dma((n_units,)),
            dma((n_units, n_run - 1)),
            dma((n_units, n_run - 1)),
            dma((n_run - 1,)),
            dma((n_run - 1,)),
            dma((n_rep - 1,)),
            dma((n_rep - 1,)),
            dma((2, n_units, n_x)),
            dma((2, n_units, n_x)),
            dma((2, n_units, n_x)),
            dma((2, n_units, n_x)),
        ],
        compiler_params=pltpu.CompilerParams(
            collective_id=0, has_side_effects=True, vmem_limit_bytes=46 * 1024 * 1024
        ),
        name="exchange_step",
    )(coef.transpose(1, 0, 2), edge_count, edge_system, edge_feats, edge_grads, weights, first_moment, second_moment)
    block = jax.ShapeDtypeStruct(weights.shape, f32)
    return pl.pallas_call(
        store_kernel,
        out_shape=(block, block, block, jax.ShapeDtypeStruct((1, nsys, local, dout), bf16)),
        in_specs=[vmem] * 4,
        out_specs=(anywhere,) * 4,
        scratch_shapes=[dma((4,))],
        compiler_params=pltpu.CompilerParams(vmem_limit_bytes=1024 * 1024),
        name="store",
    )(*(pltpu.with_memory_space_constraint(out, pltpu.VMEM) for out in outs))


def solution(mesh):
    placed = (
        P("rep", "run", None),
        P("rep", "run", None),
        P("rep", "run"),
        P("rep", "run"),
        P("rep", None, None),
        P("rep", "run", None),
        P("rep", "run", None),
        P("rep", "run", None),
    )
    return jax.shard_map(
        functools.partial(on_device, mesh.shape["run"], mesh.shape["rep"]),
        mesh=mesh,
        in_specs=placed,
        out_specs=(
            P("rep", "run", None),
            P("rep", "run", None),
            P("rep", "run", None),
            P("rep", None, "run", None),
        ),
        check_vma=False,
    )
```

time: 113 us -> 107 us (0.947)
  Pallas kernels: 110 us -> 105 us
  local copies, waits for them, and re-layouts: 1.28 us -> 0 us
    pallas_call x1, Pallas kernels: 105 us -> 101 us  [on_device(): pl.pallas_call(functools.partial(step_kernel, n_run, n_rep, nsys, held, u...]
    unnamed x1 -> x0, local copies, waits for them, and re-layouts: 1.28 us -> none
where the time goes in v2:
time: 107 us
  Pallas kernels  105 us (98%)
  between operations  1.45 us (1%)
    pallas_call x1, Pallas kernels, on_device(): pl.pallas_call(functools.partial(step_kernel, n_run, n_rep, nsys, held, u...  101 us
    pallas_call x1, Pallas kernels, on_device(): pl.pallas_call(store_kernel, out_shape=(block, block, block, jax.ShapeDty...  4.21 us

profile of v2, /device:TPU:0, one launch (start us, length us, event | category | flops | bytes accessed | tf_op | source)
XLA Modules:
  0.0 106.7 jit_solution(1718728526941383046)
XLA Ops:
  1.3 101.1 %exchange_step.1 = (f32[8,160,640]{2,1,0:T(8,128)S(1)}, f32[8,160,640]{2,1,0:T(8,128)S(1)}, f32[8,160,640]{2,1,0:T(8,128)S(1)}, bf16[6,160,640]{2,1,0:T(8,128)(2,1)S(1)}) custom-call(f32[6,1,32]{2,1,0:T(1,128)} %bitcast.1, s32[1,1]{1,0:T(1,128)S(6)} %copy.12.count, s32[1,2048]{1,0:T(1,128)} %system.1, bf16[1,2048,1280]{2,1,0:T(8,128)(2,1)} %feats.1, ...), custom_call_target="tpu_custom_call" | custom-call | tf_op jit(solution)/shard_map/exchange_step/pallas_call | solution.py:360
  102.3 4.2 %store.1 = (f32[8,160,640]{2,1,0:T(8,128)}, f32[8,160,640]{2,1,0:T(8,128)}, f32[8,160,640]{2,1,0:T(8,128)}, bf16[1,6,160,640]{3,2,1,0:T(8,128)(2,1)}) custom-call(f32[8,160,640]{2,1,0:T(8,128)S(1)} %get-tuple-element.8.w, f32[8,160,640]{2,1,0:T(8,128)S(1)} %get-tuple-element.9.f, f32[8,160,640]{2,1,0:T(8,128)S(1)} %get-tuple-element.10.s, ...), custom_call_target="tpu_custom_call" | custom-call | tf_op jit(solution)/shard_map/store/pallas_call | solution.py:398

commit v3 on v2

--- a/solution.py
+++ b/solution.py
@@ -9,6 +9,7 @@
 MESH = pl.DeviceIdType.MESH
 LANES = 128
 DEPTH = 256
+LAG = 1
 
 
 def step_kernel(
@@ -282,30 +283,30 @@
         copy.wait_recv()
 
     moved_sums, moved_new = {}, {}
-    for t in range(n_units + 3):
+    for t in range(n_units + LAG + 2):
         if t < n_units:
             pieces[t][0].wait()
             for copy in pieces[t][1:]:
                 copy.wait_recv()
         for u in due(t):
             scatter(u)
-        if 1 <= t <= n_units:
-            relay(sums, 0, t - 1, moved_sums[t - 1])
         if t < n_units:
             sum_systems(t)
             moved_sums[t] = spread(sums, 0, t)
         if 1 <= t <= n_units:
-            collect(moved_sums[t - 1])
-            if t == 1:
+            relay(sums, 0, t - 1, moved_sums[t - 1])
+        if LAG <= t < n_units + LAG:
+            collect(moved_sums[t - LAG])
+            if t == LAG:
                 for load in loads:
                     load.wait()
-            update(t - 1)
-            moved_new[t - 1] = spread(rounded, 1, t - 1)
-        if 2 <= t <= n_units + 1:
-            relay(rounded, 1, t - 2, moved_new[t - 2])
-        if t >= 3:
-            collect(moved_new[t - 3])
-            merge(t - 3)
+            update(t - LAG)
+            moved_new[t - LAG] = spread(rounded, 1, t - LAG)
+        if LAG + 1 <= t < n_units + LAG + 1:
+            relay(rounded, 1, t - LAG - 1, moved_new[t - LAG - 1])
+        if t >= LAG + 2:
+            collect(moved_new[t - LAG - 2])
+            merge(t - LAG - 2)
         for u in due(t + 1):
             prepare(u)
     for copy in started:
@@ -313,10 +314,13 @@
 
 
 def store_kernel(w, f, s, m, w_out, f_out, s_out, m_out, sems):
-    copies = [
-        pltpu.make_async_copy(src, dst, sems.at[i])
-        for i, (src, dst) in enumerate(((w, w_out), (f, f_out), (s, s_out), (m, m_out.at[0])))
-    ]
+    pairs = ((w, w_out), (f, f_out), (s, s_out), (m, m_out.at[0]))
+    copies = []
+    for i, (src, dst) in enumerate(pairs):
+        n = src.shape[0]
+        for j, (at, size) in enumerate(((0, n // 2), (n // 2, n - n // 2))):
+            part = pl.ds(at, size)
+            copies.append(pltpu.make_async_copy(src.at[part], dst.at[part], sems.at[i, j]))
     for copy in copies:
         copy.start()
     for copy in copies:
@@ -400,7 +404,7 @@
         out_shape=(block, block, block, jax.ShapeDtypeStruct((1, nsys, local, dout), bf16)),
         in_specs=[vmem] * 4,
         out_specs=(anywhere,) * 4,
-        scratch_shapes=[dma((4,))],
+        scratch_shapes=[dma((4, 2))],
         compiler_params=pltpu.CompilerParams(vmem_limit_bytes=1024 * 1024),
         name="store",
     )(*(pltpu.with_memory_space_constraint(out, pltpu.VMEM) for out in outs))

time: 107 us -> 106 us (level)
  no operation moved by 1% of the time
where the time goes in v3:
time: 106 us
  Pallas kernels  105 us (99%)
  between operations  1.45 us (1%)
    pallas_call x1, Pallas kernels, on_device(): pl.pallas_call(functools.partial(step_kernel, n_run, n_rep, nsys, held, u...  101 us
    pallas_call x1, Pallas kernels, on_device(): pl.pallas_call(store_kernel, out_shape=(block, block, block, jax.ShapeDty...  4.18 us

profile of v3, /device:TPU:0, one launch (start us, length us, event | category | flops | bytes accessed | tf_op | source)
XLA Modules:
  0.0 106.2 jit_solution(3081963020080313891)
XLA Ops:
  1.3 100.6 %exchange_step.1 = (f32[8,160,640]{2,1,0:T(8,128)S(1)}, f32[8,160,640]{2,1,0:T(8,128)S(1)}, f32[8,160,640]{2,1,0:T(8,128)S(1)}, bf16[6,160,640]{2,1,0:T(8,128)(2,1)S(1)}) custom-call(f32[6,1,32]{2,1,0:T(1,128)} %bitcast.1, s32[1,1]{1,0:T(1,128)S(6)} %copy.12.count, s32[1,2048]{1,0:T(1,128)} %system.1, bf16[1,2048,1280]{2,1,0:T(8,128)(2,1)} %feats.1, ...), custom_call_target="tpu_custom_call" | custom-call | tf_op jit(solution)/shard_map/exchange_step/pallas_call | solution.py:364
  101.9 4.2 %store.1 = (f32[8,160,640]{2,1,0:T(8,128)}, f32[8,160,640]{2,1,0:T(8,128)}, f32[8,160,640]{2,1,0:T(8,128)}, bf16[1,6,160,640]{3,2,1,0:T(8,128)(2,1)}) custom-call(f32[8,160,640]{2,1,0:T(8,128)S(1)} %get-tuple-element.8.w, f32[8,160,640]{2,1,0:T(8,128)S(1)} %get-tuple-element.9.f, f32[8,160,640]{2,1,0:T(8,128)S(1)} %get-tuple-element.10.s, ...), custom_call_target="tpu_custom_call" | custom-call | tf_op jit(solution)/shard_map/store/pallas_call | solution.py:402
